TPU v7x, 32 devices: a whole 2x2x4 slice. The times are simulated.
32 devices in a mesh: group: 4 (over y, x), member: 8 (over z, core).
Axes of the slice: x: 2, y: 2, z: 4, core: 2. Of those that a mesh axis runs over, the one named last changes fastest.
Arguments:
- factors: bfloat16 [4, 8192, 8192], P('group', 'member'), as said below
- owner: int32 [1], replicated, may hold values from 0 to 3
- grads: bfloat16 [8192, 512], P(None, 'group')
Outputs:
- new_factor: bfloat16 [8192, 8192], P('member', 'group')
Inputs may be any that keep to these rules, and one draw needn't show every extreme that they name: `owner`: index of the group that owns the updated factor. `factors`: every group's factor is upper triangular with a positive diagonal.
All inputs are finite; a program needn't handle non-finite values.
Results may differ from a plain program's by a relative error of at most 0.0061.
Values may be sent and summed in bfloat16 or wider, within the bound.
A program may use at most 192 MiB of HBM per device.

v0:
```python
import jax
import jax.numpy as jnp
from jax import lax
from jax.sharding import PartitionSpec as P

step_size = 1.0
highest = lax.Precision.HIGHEST


def from_root(value, axis, root):
    mine = lax.axis_index(axis) == root
    return lax.psum(jnp.where(mine, value, jnp.zeros_like(value)), axis)


def prefix(part, axis, combine, identity):
    count = lax.axis_size(axis)
    place = lax.axis_index(axis)
    ahead = count - 1 - place
    gathered = lax.all_gather(part, axis)
    state = jnp.zeros_like(part) + jnp.asarray(identity, part.dtype)

    def one(lap, state):
        source = count - 1 - lap
        return combine(state, lax.dynamic_index_in_dim(gathered, source, 0, False))

    return lax.fori_loop(0, ahead, one, state)


def contract_rows(left_block, right_block):
    return lax.dot_general(
        left_block, right_block, (((0,), (0,)), ((), ())), preferred_element_type=jnp.float32
    )


def add_blocks(earlier_sum, later_sum):
    return earlier_sum + later_sum


def shards(factors, owner, grads):
    local_panel = factors[0]
    factor_panel = from_root(local_panel, "group", owner[0])
    projected = jnp.dot(factor_panel, grads, preferred_element_type=jnp.float32).astype(
        jnp.bfloat16
    )
    precond = lax.psum_scatter(
        contract_rows(factor_panel, projected), "member", scatter_dimension=0, tiled=True
    ).astype(jnp.bfloat16)
    precond_wide = precond.astype(jnp.float32)
    square_total = lax.psum(jnp.sum(precond_wide * precond_wide), ("group", "member"))
    factor_order = factor_panel.shape[1]
    group_count = lax.axis_size("group")
    total_columns = precond.shape[1] * group_count
    mean_square = square_total / (factor_order * total_columns)
    step_rate = step_size / (1.0 + mean_square)
    block_width = factor_order // group_count
    group_index = lax.axis_index("group")
    own_block = lax.dynamic_slice_in_dim(factor_panel, group_index * block_width, block_width, 1)
    left_rows = lax.all_gather(precond, "group", axis=1, tiled=True)
    partial_terms = contract_rows(left_rows, own_block)
    tail_total = prefix(partial_terms, "member", add_blocks, jnp.zeros_like(partial_terms))
    diagonal_gram = jnp.triu(jnp.dot(left_rows, left_rows.T, preferred_element_type=jnp.float32))
    combined = jnp.dot(left_rows.astype(jnp.float32), tail_total, precision=highest)
    combined = combined + jnp.dot(diagonal_gram, own_block.astype(jnp.float32), precision=highest)
    updated = (1.0 + step_rate) * own_block.astype(
        jnp.float32
    ) - step_rate / total_columns * combined
    return updated.astype(jnp.bfloat16)


def solution(mesh):
    in_specs = (P("group", "member", None), P(), P(None, "group"))
    out_specs = P("member", "group")
    return jax.shard_map(shards, mesh=mesh, in_specs=in_specs, out_specs=out_specs, check_vma=False)
```

profile of v0, /device:TPU:0, one launch (start us, length us, event | category | flops | bytes accessed | tf_op | source)
XLA Modules:
  0.0 802.5 jit_solution(13536739586304521661)
XLA Ops:
  6.5 0.0 copy-start
  6.5 0.0 all-reduce.2.cloned.1.call-start
  7.3 13.8 %select_bitcast_fusion = bf16[1024,8192]{1,0:T(8,128)(2,1)} fusion(bf16[1,1024,8192]{2,1,0:T(8,128)(2,1)} %param.5, pred[]{:T(512)S(6)} %eq.3), kind=kLoop, calls=%fused_computation.1 | loop fusion | flops 8388608 | bytes 33554432 | tf_op jit(solution)/shard_map/jit(_where)/select_n | solution.py:12
  21.1 0.0 all-reduce.2.cloned.1.call-update
  21.1 0.0 reduce-scatter.2.cloned.1.call-start
  21.2 308.3 %all-reduce.2.cloned.1.call-done = bf16[1024,8192]{1,0:T(8,128)(2,1)} async-done(((bf16[1024,8192]{1,0:T(8,128)(2,1)}), bf16[1024,8192]{1,0:T(8,128)(2,1)}) %all-reduce.2.cloned.1.call-update) | async-done | bytes 16777232 | tf_op jit(solution)/shard_map/psum | solution.py:12
  329.5 0.0 copy-done
  329.5 29.9 %fusion.10 = f32[8192,128]{1,0:T(8,128)} fusion(bf16[1024,8192]{1,0:T(8,128)(2,1)} %all-reduce.2.cloned.1.call-done, bf16[8192,128]{1,0:T(8,128)(2,1)S(1)} %copy-done), kind=kOutput, calls=%fused_computation.17 | convolution fusion | flops 4295098368 | bytes 23068672 | tf_op jit(solution)/shard_map/dot_general | solution.py:30
  359.3 0.0 reduce-scatter.2.cloned.1.call-update
  359.4 0.0 all-gather.4.cloned.1.call-start
  359.4 51.1 %reduce-scatter.2.cloned.1.call-done = f32[1024,128]{1,0:T(8,128)} async-done(((f32[8192,128]{1,0:T(8,128)}), f32[1024,128]{1,0:T(8,128)}) %reduce-scatter.2.cloned.1.call-update) | async-done | bytes 524304 | tf_op jit(solution)/shard_map/reduce_scatter | solution.py:45
  410.5 2.4 multiply_reduce_fusion
  412.9 0.0 all-gather.4.cloned.1.call-update
  412.9 0.0 all-gather.6.cloned.1.call-start
  413.0 24.9 %all-gather.4.cloned.1.call-done = bf16[1024,512]{1,0:T(8,128)(2,1)} async-done(((bf16[1024,128]{1,0:T(8,128)(2,1)}), bf16[1024,512]{1,0:T(8,128)(2,1)}) %all-gather.4.cloned.1.call-update) | async-done | bytes 1048592 | tf_op jit(solution)/shard_map/all_gather | solution.py:58
  437.9 6.9 fusion.3
  444.8 0.0 copy-start.2
  444.8 0.0 all-gather.6.cloned.1.call-update
  444.9 51.4 %psum.15 = f32[]{:T(128)} all-reduce(f32[]{:T(128)} %get-tuple-element.70), channel_id=1, replica_groups=mesh['group'=4,'member'=8] {'group','member'}, use_global_device_ids=true, to_apply=%region_3.4 | all-reduce | flops 1 | bytes 8 | tf_op jit(solution)/shard_map/psum | solution.py:49
  497.0 0.0 copy-done.2
  497.1 1.3 fusion.11
  498.3 17.2 %fusion = f32[1024,2048]{1,0:T(8,128)} fusion(f32[1024,1024]{1,0:T(8,128)S(1)} %fusion.11, bf16[1024,8192]{1,0:T(8,128)(2,1)} %all-reduce.2.cloned.1.call-done, s32[]{:T(128)S(6)} %select_n.28, s32[1024]{0:T(1024)S(1)} %iota_add_fusion), kind=kOutput, calls=%fused_computation.3 | convolution fusion | flops 25771900928 | bytes 16781316 | tf_op jit(solution)/shard_map/dot_general | solution.py:63
  515.5 219.1 %all-gather.6.cloned.1.call-done = f32[4096,2048]{1,0:T(8,128)} async-done(((f32[512,2048]{1,0:T(8,128)}), f32[4096,2048]{1,0:T(8,128)}) %all-gather.6.cloned.1.call-update) | async-done | bytes 33554448 | tf_op jit(solution)/shard_map/all_gather | solution.py:19
  734.7 2.4 broadcast_in_dim.11
  737.1 45.4 %while.12 = (s32[]{:T(128)}, f32[512,2048]{1,0:T(8,128)}, s32[]{:T(128)}, f32[8,512,2048]{2,1,0:T(8,128)}, s32[]{:T(128)}, /*index=5*/s32[]{:T(128)}, s32[]{:T(128)}, s32[]{:T(128)}) while((s32[]{:T(128)}, f32[512,2048]{1,0:T(8,128)}, s32[]{:T(128)}, f32[8,512,2048]{2,1,0:T(8,128)}, s32[]{:T(128)}, /*index=5*/s32[]{:T(128)}, s32[]{:T(128)}, ...), condition=%wide.region_5.6_spmd, body=%wide.region_4.5_spmd.sunk | while | flops 1048582 | bytes 12583047 | solution.py:26
  737.1 6.5 bitcast_add_fusion.2
  743.6 6.5 bitcast_add_fusion.2
  750.1 6.5 bitcast_add_fusion.2
  756.6 6.5 bitcast_add_fusion.2
  763.0 6.5 bitcast_add_fusion.2
  769.5 6.5 bitcast_add_fusion.2
  776.0 6.5 bitcast_add_fusion.2
  782.5 0.0 copy-start.1
  782.5 13.5 %subtract_convert_fusion = bf16[1024,2048]{1,0:T(8,128)(2,1)} fusion(f32[1024,2048]{1,0:T(8,128)} %fusion, f32[]{:T(128)S(6)} %div.11, f32[]{:T(128)S(6)} %add.47, bf16[1024,512]{1,0:T(8,128)(2,1)S(1)} %copy-done.2, f32[512,2048]{1,0:T(8,128)} %get-tuple-element.61, bf16[1024,8192]{1,0:T(8,128)(2,1)} %all-reduce.2.cloned.1.call-done, s32[]{:T(128)S(6)} %select_n.28), kind=kOutput, calls=%fused_computation.2 | convolution fusion | flops 12897484800 | bytes 22020108 | tf_op jit(solution)/shard_map/dot_general | solution.py:62
  796.0 0.0 copy-done.1
  (1 shorter events, 0.0 us)
Async XLA Ops:
  6.5 322.9 %copy-start = (bf16[8192,128]{1,0:T(8,128)(2,1)S(1)}, bf16[8192,128]{1,0:T(8,128)(2,1)}, u32[]{:S(2)}) copy-start(bf16[8192,128]{1,0:T(8,128)(2,1)} %param.7) | copy-start | bytes 6291460
  6.5 322.9 %all-reduce.2.cloned.1.call-start = ((), (), s32[]{:S(2)}) async-start(), calls=%async_computation.1 | async-start | bytes 33554432 | tf_op jit(solution)/shard_map/psum | solution.py:12
  21.1 389.4 %reduce-scatter.2.cloned.1.call-start = ((), (), s32[]{:S(2)}) async-start(), calls=%async_computation.2 | async-start | bytes 4718592 | tf_op jit(solution)/shard_map/reduce_scatter | solution.py:45
  359.4 78.6 %all-gather.4.cloned.1.call-start = ((), (), s32[]{:S(2)}) async-start(), calls=%async_computation.3 | async-start | bytes 1310720 | tf_op jit(solution)/shard_map/all_gather | solution.py:58
  412.9 321.7 %all-gather.6.cloned.1.call-start = ((), (), s32[]{:S(2)}) async-start(), calls=%async_computation.4 | async-start | bytes 37748736 | tf_op jit(solution)/shard_map/all_gather | solution.py:19
  444.8 52.2 %copy-start.2 = (bf16[1024,512]{1,0:T(8,128)(2,1)S(1)}, bf16[1024,512]{1,0:T(8,128)(2,1)}, u32[]{:S(2)}) copy-start(bf16[1024,512]{1,0:T(8,128)(2,1)} %all-gather.4.cloned.1.call-done) | copy-start | bytes 3145732
  782.5 13.5 %copy-start.1 = (bf16[8192,128]{1,0:T(8,128)(2,1)S(1)}, bf16[8192,128]{1,0:T(8,128)(2,1)}, u32[]{:S(2)}) copy-start(bf16[8192,128]{1,0:T(8,128)(2,1)} %param.7) | copy-start | bytes 6291460
Sparse Core Ops, SparseCore 0:
  21.3 308.1 all-reduce.1
  359.5 50.9 reduce-scatter.1
  413.1 24.8 all-gather.3
  445.0 289.6 all-gather.5
where the time goes:
time: 803 us; the launch traced here: 802 us
  waiting for transfers between devices  603 us (75%)
  matrix products  68.7 us (9%)
  other arithmetic  61.6 us (8%)
  blocking collectives  51.4 us (6%)
  between operations  14.7 us (2%)
    psum x1, waiting for transfers between devices, from_root(): return lax.psum(jnp.where(mine, value, jnp.zeros_like(value)), axis)  308 us
    all_gather x1, waiting for transfers between devices, prefix(): gathered = lax.all_gather(part, axis)  219 us
    psum x1, blocking collectives, shards(): lax.psum(jnp.sum(precond_wide * precond_wide), ('group', 'member'))  51.4 us
    reduce_scatter x1, waiting for transfers between devices, shards(): lax.psum_scatter(contract_rows(factor_panel, projected), 'member', scatte...  51.1 us
    add x7, other arithmetic, add_blocks(): return earlier_sum + later_sum  45.4 us
    dot_general x2, matrix products, contract_rows(): lax.dot_general(left_block, right_block, (((0,), (0,)), ((), ())), prefer...  36.8 us
    all_gather x1, waiting for transfers between devices, shards(): left_rows = lax.all_gather(precond, 'group', axis=1, tiled=True)  24.9 us
    dot_general x1, matrix products, shards(): jnp.dot(diagonal_gram, own_block.astype(jnp.float32), precision=highest)  17.2 us
  transfers between devices with their start and end apart: 4, of which 4 were waited for; matrix products, arithmetic and copies ran while one was open for 2% of the time, Pallas kernels for 0%

commit v1 on v0

--- a/solution.py
+++ b/solution.py
@@ -9,7 +9,7 @@
 
 def from_root(value, axis, root):
     mine = lax.axis_index(axis) == root
-    return lax.psum(jnp.where(mine, value, jnp.zeros_like(value)), axis)
+    return jnp.sum(lax.all_gather(jnp.where(mine, value, jnp.zeros_like(value)), axis), axis=0)
 
 
 def prefix(part, axis, combine, identity):

time: 803 us -> 1100 us (1.37)
  waiting for transfers between devices: 603 us -> 872 us
  other arithmetic: 61.6 us -> 91.9 us
    all_gather x0 -> x1, waiting for transfers between devices: none -> 578 us  [from_root(): lax.all_gather(jnp.where(mine, value, jnp.zeros_like(value)), axis)]
    psum x1 -> x0, waiting for transfers between devices: 308 us -> none  [from_root(): return lax.psum(jnp.where(mine, value, jnp.zeros_like(value)), axis)]
    reduce_sum x0 -> x1, other arithmetic: none -> 30.3 us  [from_root(): jnp.sum(lax.all_gather(jnp.where(mine, value, jnp.zeros_like(value)), axi...]
where the time goes in v1:
time: 1100 us
  waiting for transfers between devices  872 us (79%)
  other arithmetic  91.9 us (8%)
  matrix products  68.9 us (6%)
  blocking collectives  51.4 us (5%)
  between operations  14.6 us (1%)
    all_gather x1, waiting for transfers between devices, from_root(): lax.all_gather(jnp.where(mine, value, jnp.zeros_like(value)), axis)  578 us
    all_gather x1, waiting for transfers between devices, prefix(): gathered = lax.all_gather(part, axis)  219 us
    psum x1, blocking collectives, shards(): lax.psum(jnp.sum(precond_wide * precond_wide), ('group', 'member'))  51.4 us
    reduce_scatter x1, waiting for transfers between devices, shards(): lax.psum_scatter(contract_rows(factor_panel, projected), 'member', scatte...  50 us
    add x7, other arithmetic, add_blocks(): return earlier_sum + later_sum  45.3 us
    dot_general x2, matrix products, contract_rows(): lax.dot_general(left_block, right_block, (((0,), (0,)), ((), ())), prefer...  36.9 us
    reduce_sum x1, other arithmetic, from_root(): jnp.sum(lax.all_gather(jnp.where(mine, value, jnp.zeros_like(value)), axi...  30.3 us
    all_gather x1, waiting for transfers between devices, shards(): left_rows = lax.all_gather(precond, 'group', axis=1, tiled=True)  24.8 us
  transfers between devices with their start and end apart: 4, of which 4 were waited for; matrix products, arithmetic and copies ran while one was open for 2% of the time, Pallas kernels for 0%

profile of v1, /device:TPU:0, one launch (start us, length us, event | category | flops | bytes accessed | tf_op | source)
XLA Modules:
  0.0 1101.2 jit_solution(9943110504875772924)
XLA Ops:
  6.5 0.0 copy-start
  6.5 0.0 all-gather.5.cloned.1.call-start
  7.3 13.8 %broadcast_select_fusion = bf16[1,1024,8192]{2,1,0:T(8,128)(2,1)} fusion(bf16[1,1024,8192]{2,1,0:T(8,128)(2,1)} %param.5, pred[]{:T(512)S(6)} %eq.3), kind=kLoop, calls=%fused_computation.1 | loop fusion | flops 8388608 | bytes 33554432 | tf_op jit(solution)/shard_map/jit(_where)/select_n | solution.py:12
  21.1 0.0 all-gather.5.cloned.1.call-update
  21.2 0.0 reduce-scatter.2.cloned.1.call-start
  21.2 577.6 %all-gather.5.cloned.1.call-done = bf16[4,1024,8192]{2,1,0:T(8,128)(2,1)} async-done(((bf16[1,1024,8192]{2,1,0:T(8,128)(2,1)}), bf16[4,1024,8192]{2,1,0:T(8,128)(2,1)}) %all-gather.5.cloned.1.call-update) | async-done | bytes 67108880 | tf_op jit(solution)/shard_map/all_gather | solution.py:12
  598.8 30.3 %reduce_sum.21 = bf16[1024,8192]{1,0:T(8,128)(2,1)} reduce(bf16[4,1024,8192]{2,1,0:T(8,128)(2,1)} %all-gather.5.cloned.1.call-done, bf16[]{:T(256)} %constant.49.clone.1), dimensions={0}, to_apply=%region_0.1 | reduce | flops 25165824 | bytes 83886080 | tf_op jit(solution)/shard_map/reduce_sum | solution.py:12
  629.1 0.0 copy-done
  629.1 30.0 %fusion.10 = f32[8192,128]{1,0:T(8,128)} fusion(bf16[1024,8192]{1,0:T(8,128)(2,1)} %reduce_sum.21, bf16[8192,128]{1,0:T(8,128)(2,1)S(1)} %copy-done), kind=kOutput, calls=%fused_computation.17 | convolution fusion | flops 4295098368 | bytes 23068672 | tf_op jit(solution)/shard_map/dot_general | solution.py:30
  659.2 0.0 reduce-scatter.2.cloned.1.call-update
  659.2 0.0 all-gather.7.cloned.1.call-start
  659.2 50.0 %reduce-scatter.2.cloned.1.call-done = f32[1024,128]{1,0:T(8,128)} async-done(((f32[8192,128]{1,0:T(8,128)}), f32[1024,128]{1,0:T(8,128)}) %reduce-scatter.2.cloned.1.call-update) | async-done | bytes 524304 | tf_op jit(solution)/shard_map/reduce_scatter | solution.py:45
  709.2 2.4 multiply_reduce_fusion
  711.6 0.0 all-gather.7.cloned.1.call-update
  711.7 0.2 all-gather.9.cloned.1.call-start
  711.9 24.8 %all-gather.7.cloned.1.call-done = bf16[1024,512]{1,0:T(8,128)(2,1)} async-done(((bf16[1024,128]{1,0:T(8,128)(2,1)}), bf16[1024,512]{1,0:T(8,128)(2,1)}) %all-gather.7.cloned.1.call-update) | async-done | bytes 1048592 | tf_op jit(solution)/shard_map/all_gather | solution.py:58
  736.7 6.9 fusion.3
  743.6 0.0 copy-start.2
  743.6 0.0 all-gather.9.cloned.1.call-update
  743.6 51.4 %psum.7 = f32[]{:T(128)} all-reduce(f32[]{:T(128)} %get-tuple-element.70), channel_id=1, replica_groups=mesh['group'=4,'member'=8] {'group','member'}, use_global_device_ids=true, to_apply=%region_3.4 | all-reduce | flops 1 | bytes 8 | tf_op jit(solution)/shard_map/psum | solution.py:49
  795.7 0.0 copy-done.2
  795.7 1.3 fusion.11
  797.0 17.2 %fusion = f32[1024,2048]{1,0:T(8,128)} fusion(f32[1024,1024]{1,0:T(8,128)S(1)} %fusion.11, bf16[1024,8192]{1,0:T(8,128)(2,1)} %reduce_sum.21, s32[]{:T(128)S(6)} %select_n.25, s32[1024]{0:T(1024)S(1)} %iota_add_fusion), kind=kOutput, calls=%fused_computation.3 | convolution fusion | flops 25771900928 | bytes 16781316 | tf_op jit(solution)/shard_map/dot_general | solution.py:63
  814.2 219.1 %all-gather.9.cloned.1.call-done = f32[4096,2048]{1,0:T(8,128)} async-done(((f32[512,2048]{1,0:T(8,128)}), f32[4096,2048]{1,0:T(8,128)}) %all-gather.9.cloned.1.call-update) | async-done | bytes 33554448 | tf_op jit(solution)/shard_map/all_gather | solution.py:19
  1033.4 2.4 broadcast_in_dim.11
  1035.8 45.3 %while.12 = (s32[]{:T(128)}, f32[512,2048]{1,0:T(8,128)}, s32[]{:T(128)}, f32[8,512,2048]{2,1,0:T(8,128)}, s32[]{:T(128)}, /*index=5*/s32[]{:T(128)}, s32[]{:T(128)}, s32[]{:T(128)}) while((s32[]{:T(128)}, f32[512,2048]{1,0:T(8,128)}, s32[]{:T(128)}, f32[8,512,2048]{2,1,0:T(8,128)}, s32[]{:T(128)}, /*index=5*/s32[]{:T(128)}, s32[]{:T(128)}, ...), condition=%wide.region_5.6_spmd, body=%wide.region_4.5_spmd.sunk | while | flops 1048582 | bytes 12583047 | solution.py:26
  1035.8 6.5 bitcast_add_fusion.2
  1042.3 6.5 bitcast_add_fusion.2
  1048.8 6.5 bitcast_add_fusion.2
  1055.2 6.5 bitcast_add_fusion.2
  1061.7 6.5 bitcast_add_fusion.2
  1068.2 6.5 bitcast_add_fusion.2
  1074.7 6.5 bitcast_add_fusion.2
  1081.1 0.0 copy-start.1
  1081.1 13.5 %subtract_convert_fusion = bf16[1024,2048]{1,0:T(8,128)(2,1)} fusion(f32[1024,2048]{1,0:T(8,128)} %fusion, f32[]{:T(128)S(6)} %div.11, f32[]{:T(128)S(6)} %add.45, bf16[1024,512]{1,0:T(8,128)(2,1)S(1)} %copy-done.2, f32[512,2048]{1,0:T(8,128)} %get-tuple-element.61, bf16[1024,8192]{1,0:T(8,128)(2,1)} %reduce_sum.21, s32[]{:T(128)S(6)} %select_n.25), kind=kOutput, calls=%fused_computation.2 | convolution fusion | flops 12897484800 | bytes 22020108 | tf_op jit(solution)/shard_map/dot_general | solution.py:62
  1094.6 0.0 copy-done.1
  (1 shorter events, 0.0 us)
Async XLA Ops:
  6.5 622.6 %copy-start = (bf16[8192,128]{1,0:T(8,128)(2,1)S(1)}, bf16[8192,128]{1,0:T(8,128)(2,1)}, u32[]{:S(2)}) copy-start(bf16[8192,128]{1,0:T(8,128)(2,1)} %param.7) | copy-start | bytes 6291460
  6.5 592.3 %all-gather.5.cloned.1.call-start = ((), (), s32[]{:S(2)}) async-start(), calls=%async_computation.1 | async-start | bytes 83886080 | tf_op jit(solution)/shard_map/all_gather | solution.py:12
  21.2 688.1 %reduce-scatter.2.cloned.1.call-start = ((), (), s32[]{:S(2)}) async-start(), calls=%async_computation.2 | async-start | bytes 4718592 | tf_op jit(solution)/shard_map/reduce_scatter | solution.py:45
  659.2 77.5 %all-gather.7.cloned.1.call-start = ((), (), s32[]{:S(2)}) async-start(), calls=%async_computation.3 | async-start | bytes 1310720 | tf_op jit(solution)/shard_map/all_gather | solution.py:58
  711.7 321.7 %all-gather.9.cloned.1.call-start = ((), (), s32[]{:S(2)}) async-start(), calls=%async_computation.4 | async-start | bytes 37748736 | tf_op jit(solution)/shard_map/all_gather | solution.py:19
  743.6 52.2 %copy-start.2 = (bf16[1024,512]{1,0:T(8,128)(2,1)S(1)}, bf16[1024,512]{1,0:T(8,128)(2,1)}, u32[]{:S(2)}) copy-start(bf16[1024,512]{1,0:T(8,128)(2,1)} %all-gather.7.cloned.1.call-done) | copy-start | bytes 3145732
  1081.1 13.5 %copy-start.1 = (bf16[8192,128]{1,0:T(8,128)(2,1)S(1)}, bf16[8192,128]{1,0:T(8,128)(2,1)}, u32[]{:S(2)}) copy-start(bf16[8192,128]{1,0:T(8,128)(2,1)} %param.7) | copy-start | bytes 6291460
Sparse Core Ops, SparseCore 0:
  21.3 577.4 all-gather.4
  659.3 49.8 reduce-scatter.1
  711.8 24.8 all-gather.6
  743.7 289.5 all-gather.8
